TPU v7x, 32 devices: a whole 2x2x4 slice. The times are simulated.
32 devices in a mesh: replica: 4 (over x, core), fsdp: 8 (over z, y).
Axes of the slice: x: 2, y: 2, z: 4, core: 2. Of those that a mesh axis runs over, the one named last changes fastest.
Arguments:
- byte_input: bfloat16 [32768, 768], P(('replica', 'fsdp')), may hold values from -6 to 6
- global_out: bfloat16 [32768, 768], P(('replica', 'fsdp')), may hold values from -6 to 6
- cotangent: bfloat16 [32768, 768], P(('replica', 'fsdp')), may hold values from -6 to 6
- seq_patches: int32 [4, 4], P('replica'), may hold values from 1 to 512, 1024 in all within a row
- last_fill: int32 [4, 4], P('replica'), may hold values from 1 to 8
- deal_slots: int32 [4, 1024], P('replica', 'fsdp'), may hold values from 0 to 1023, as said below
- first_gain: bfloat16 [768], P('fsdp'), may hold values from 0.5 to 1.5
- first_shift: bfloat16 [768], P('fsdp'), may hold values from -1.796875 to 1.796875
- qkv_weight: bfloat16 [768, 2304], P('fsdp'), may hold values from -0.21875 to 0.21875
- out_weight: bfloat16 [768, 768], P('fsdp'), may hold values from -0.4375 to 0.4375
- second_gain: bfloat16 [768], P('fsdp'), may hold values from 0.5 to 1.5
- second_shift: bfloat16 [768], P('fsdp'), may hold values from -1.796875 to 1.796875
- up_weight: bfloat16 [768, 3072], P('fsdp'), may hold values from -0.21875 to 0.21875
- up_bias: bfloat16 [3072], P('fsdp'), may hold values from -3 to 3
- down_weight: bfloat16 [3072, 768], P('fsdp'), may hold values from -0.15625 to 0.15625
- down_bias: bfloat16 [768], P('fsdp'), may hold values from -1.796875 to 1.796875
Outputs:
- layer_out: bfloat16 [32768, 768], P(('replica', 'fsdp'))
- grad_input: bfloat16 [32768, 768], P(('replica', 'fsdp'))
- grad_global: bfloat16 [32768, 768], P(('replica', 'fsdp'))
- grad_first_gain: float32 [768], P('fsdp')
- grad_first_shift: float32 [768], P('fsdp')
- grad_qkv_weight: float32 [768, 2304], P('fsdp')
- grad_out_weight: float32 [768, 768], P('fsdp')
- grad_second_gain: float32 [768], P('fsdp')
- grad_second_shift: float32 [768], P('fsdp')
- grad_up_weight: float32 [768, 3072], P('fsdp')
- grad_up_bias: float32 [3072], P('fsdp')
- grad_down_weight: float32 [3072, 768], P('fsdp')
- grad_down_bias: float32 [768], P('fsdp')
Inputs may be any that keep to these rules, and one draw needn't show every extreme that they name: `seq_patches`: row g gives the patches of the 4 sequences of group g in order; each row sums to 1024 and its largest entry is 512. `last_fill`: bytes used in the last patch of each sequence; the rest of that patch is padding. Each row is a permutation of 0 to 1023. Of the patches p in any aligned block of 128, exactly 16 have deal_slots in each aligned block of 128 positions.
All inputs are finite; a program needn't handle non-finite values.
Results may differ from a plain program's by a relative error of at most 0.017.
Values may be sent and summed in bfloat16 or wider, within the bound.
No kernel may reach another device: no remote copies, remote signals or barrier semaphores. Data moves between devices by JAX's collectives and lax.ppermute only.
A program may use at most 128 MiB of HBM per device.

v0:
```python
import jax
import jax.numpy as jnp
from jax import lax
from jax.sharding import PartitionSpec as P

HEADS = 12
HEAD_DIM = 64
PATCH = 8
EPSILON = 1e-05


def contract_rows(left, right):
    return lax.dot_general(
        left, right, (((0,), (0,)), ((), ())), preferred_element_type=jnp.float32
    )


def contract_cols(left, right):
    return lax.dot_general(
        left, right, (((1,), (1,)), ((), ())), preferred_element_type=jnp.float32
    )


def apply_layer_normalize(values, gain, shift):
    center = values - jnp.mean(values, axis=1, keepdims=True)
    inverse = lax.rsqrt(jnp.mean(jnp.square(center), axis=1, keepdims=True) + EPSILON)
    normed = center * inverse
    return (normed * gain + shift, normed, inverse)


def normalize_pullback(upstream, gain, normed, inverse):
    scaled = upstream * gain
    inner = (
        scaled
        - jnp.mean(scaled, axis=1, keepdims=True)
        - normed * jnp.mean(scaled * normed, axis=1, keepdims=True)
    )
    return (inverse * inner, jnp.sum(upstream * normed, axis=0), jnp.sum(upstream, axis=0))


def block_mask(span):
    index = jnp.arange(span, dtype=jnp.int32)
    return (index[:, None] // PATCH == index[None, :] // PATCH) & (index[None, :] <= index[:, None])


def attention_scores(queries, keys_part, allowed):
    raw = jnp.einsum(
        "gqhd,gkhd->ghqk", queries, keys_part, preferred_element_type=jnp.float32
    ) * HEAD_DIM ** (-0.5)
    return jnp.where(allowed, raw, -1e30)


def body(
    byte_input,
    global_out,
    cotangent,
    seq_patches,
    last_fill,
    deal_slots,
    first_gain,
    first_shift,
    qkv_weight,
    out_weight,
    second_gain,
    second_shift,
    up_weight,
    up_bias,
    down_weight,
    down_bias,
):
    row_count = byte_input.shape[0]
    model_width = byte_input.shape[1]
    patch_count = row_count // PATCH
    fsdp_count = lax.axis_size("fsdp")
    share = patch_count // fsdp_count
    patch_ids = lax.axis_index("fsdp") * patch_count + jnp.arange(patch_count, dtype=jnp.int32)
    seq_ends = jnp.cumsum(seq_patches[0])
    seq_ids = jnp.sum((patch_ids[:, None] >= seq_ends[None, :]).astype(jnp.int32), axis=1)
    seq_hits = (seq_ids[:, None] == jnp.arange(seq_ends.shape[0], dtype=jnp.int32)[None, :]).astype(
        jnp.int32
    )
    end_of = jnp.sum(seq_hits * seq_ends[None, :], axis=1)
    fill_of = jnp.sum(seq_hits * last_fill[0][None, :], axis=1)
    in_patch = jnp.arange(PATCH, dtype=jnp.int32)
    keep_byte = (
        (patch_ids != end_of - 1)[:, None] | (in_patch[None, :] < fill_of[:, None])
    ).reshape(row_count, 1)
    target = deal_slots[0] // patch_count
    dealt_slot = deal_slots[0] % patch_count
    dest_hits = (target[:, None] == jnp.arange(fsdp_count, dtype=jnp.int32)[None, :]).astype(
        jnp.int32
    )
    dest_rank = jnp.sum((jnp.cumsum(dest_hits, axis=0) - 1) * dest_hits, axis=1)
    send_place = target * share + dest_rank
    send_order = (
        jnp.zeros((patch_count,), jnp.int32)
        .at[send_place]
        .set(jnp.arange(patch_count, dtype=jnp.int32))
    )

    def pack_rows(values):
        return values.reshape(patch_count, PATCH, model_width)[send_order].reshape(
            row_count, model_width
        )

    def unpack_rows(values):
        return values.reshape(patch_count, PATCH, model_width)[send_place].reshape(
            row_count, model_width
        )

    arrived, arrived_slot = (
        lax.all_to_all(pack_rows(byte_input), "fsdp", split_axis=0, concat_axis=0, tiled=True),
        lax.all_to_all(dealt_slot[send_order], "fsdp", split_axis=0, concat_axis=0, tiled=True),
    )
    (
        gain_full,
        complete_shift_vector,
        qkv_full,
        outproj_full,
        gain_later,
        deferred_shift_vector,
        expand_full,
        expand_bias,
        reduce_full,
        reduce_bias,
    ) = (
        lax.all_gather(first_gain, "fsdp", axis=0, tiled=True),
        lax.all_gather(first_shift, "fsdp", axis=0, tiled=True),
        lax.all_gather(qkv_weight, "fsdp", axis=0, tiled=True),
        lax.all_gather(out_weight, "fsdp", axis=0, tiled=True),
        lax.all_gather(second_gain, "fsdp", axis=0, tiled=True),
        lax.all_gather(second_shift, "fsdp", axis=0, tiled=True),
        lax.all_gather(up_weight, "fsdp", axis=0, tiled=True),
        lax.all_gather(up_bias, "fsdp", axis=0, tiled=True),
        lax.all_gather(down_weight, "fsdp", axis=0, tiled=True),
        lax.all_gather(down_bias, "fsdp", axis=0, tiled=True),
    )
    attention_norm_gain = gain_full.astype(jnp.float32)
    feedforward_norm_gain = gain_later.astype(jnp.float32)
    global_rows = global_out.reshape(patch_count, PATCH, model_width)[arrived_slot].reshape(
        row_count, model_width
    )
    residual_input = arrived.astype(jnp.float32) + global_rows.astype(jnp.float32)
    attention_normed_input, attention_centered_scaled, attention_inverse_deviation = (
        apply_layer_normalize(
            residual_input, attention_norm_gain, complete_shift_vector.astype(jnp.float32)
        )
    )
    first_in = attention_normed_input.astype(jnp.bfloat16)
    qkv_rows = jnp.dot(first_in, qkv_full, preferred_element_type=jnp.float32).astype(jnp.bfloat16)
    blocks = row_count // 128

    def heads_of(values, start):
        return lax.slice_in_dim(values, start, start + model_width, axis=1).reshape(
            blocks, 128, HEADS, HEAD_DIM
        )

    queries = heads_of(qkv_rows, 0)
    keys_part = heads_of(qkv_rows, model_width)
    values_part = heads_of(qkv_rows, 2 * model_width)
    allowed = block_mask(128)
    scores = attention_scores(queries, keys_part, allowed)
    top_score = jnp.max(scores, axis=3, keepdims=True)
    expo = jnp.exp(scores - top_score)
    total = jnp.sum(expo, axis=3, keepdims=True)
    log_total = top_score + jnp.log(total)
    probs = (expo / total).astype(jnp.bfloat16)
    mixed = jnp.einsum("ghqk,gkhd->gqhd", probs, values_part, preferred_element_type=jnp.float32)
    attended = mixed.reshape(row_count, model_width).astype(jnp.bfloat16)
    residual_midway = residual_input + jnp.dot(
        attended, outproj_full, preferred_element_type=jnp.float32
    )
    feedforward_normed_input, feedforward_centered_scaled, feedforward_inverse_deviation = (
        apply_layer_normalize(
            residual_midway, feedforward_norm_gain, deferred_shift_vector.astype(jnp.float32)
        )
    )
    second_in = feedforward_normed_input.astype(jnp.bfloat16)
    pre_act = jnp.dot(
        second_in, expand_full, preferred_element_type=jnp.float32
    ) + expand_bias.astype(jnp.float32)
    activ = jax.nn.gelu(pre_act, approximate=False).astype(jnp.bfloat16)
    result = (
        residual_midway
        + jnp.dot(activ, reduce_full, preferred_element_type=jnp.float32)
        + reduce_bias.astype(jnp.float32)
    )
    returned = lax.all_to_all(
        result.astype(jnp.bfloat16), "fsdp", split_axis=0, concat_axis=0, tiled=True
    )
    layer_out = jnp.where(keep_byte, unpack_rows(returned), jnp.zeros((), jnp.bfloat16))
    masked_cot = jnp.where(keep_byte, cotangent, jnp.zeros((), jnp.bfloat16))
    upstream_b = lax.all_to_all(
        pack_rows(masked_cot), "fsdp", split_axis=0, concat_axis=0, tiled=True
    )
    upstream = upstream_b.astype(jnp.float32)
    grad_reduce_bias = jnp.sum(upstream, axis=0)
    grad_reduce = contract_rows(activ, upstream_b)
    grad_activ = contract_cols(upstream_b, reduce_full)
    density = jnp.exp(-0.5 * jnp.square(pre_act)) * 0.3989422804014327
    cumulative = 0.5 * (1.0 + jax.scipy.special.erf(pre_act * 0.7071067811865476))
    grad_pre = (grad_activ * (cumulative + pre_act * density)).astype(jnp.bfloat16)
    grad_expand_bias = jnp.sum(grad_pre.astype(jnp.float32), axis=0)
    grad_expand = contract_rows(second_in, grad_pre)
    gradient_feedforward_branch = contract_cols(grad_pre, expand_full)
    normalize_piece, gradient_feedforward_gain, gradient_feedforward_shift = normalize_pullback(
        gradient_feedforward_branch,
        feedforward_norm_gain,
        feedforward_centered_scaled,
        feedforward_inverse_deviation,
    )
    grad_middle = upstream + normalize_piece
    grad_branch = grad_middle.astype(jnp.bfloat16)
    grad_outproj = contract_rows(attended, grad_branch)
    grad_attended = (
        contract_cols(grad_branch, outproj_full)
        .astype(jnp.bfloat16)
        .reshape(blocks, 128, HEADS, HEAD_DIM)
    )
    scores_again = attention_scores(queries, keys_part, allowed)
    probs_again = jnp.exp(scores_again - log_total)
    grad_probs = jnp.einsum(
        "gqhd,gkhd->ghqk", grad_attended, values_part, preferred_element_type=jnp.float32
    )
    grad_values = jnp.einsum(
        "ghqk,gqhd->gkhd",
        probs_again.astype(jnp.bfloat16),
        grad_attended,
        preferred_element_type=jnp.float32,
    )
    grad_scores = (
        probs_again * (grad_probs - jnp.sum(probs_again * grad_probs, axis=3, keepdims=True))
    ).astype(jnp.bfloat16)
    grad_queries = jnp.einsum(
        "ghqk,gkhd->gqhd", grad_scores, keys_part, preferred_element_type=jnp.float32
    ) * HEAD_DIM ** (-0.5)
    grad_keys = jnp.einsum(
        "ghqk,gqhd->gkhd", grad_scores, queries, preferred_element_type=jnp.float32
    ) * HEAD_DIM ** (-0.5)
    grad_qkv = jnp.concatenate(
        [
            grad_queries.reshape(row_count, model_width),
            grad_keys.reshape(row_count, model_width),
            grad_values.reshape(row_count, model_width),
        ],
        axis=1,
    ).astype(jnp.bfloat16)
    grad_qkv_full = contract_rows(first_in, grad_qkv)
    gradient_attention_branch = contract_cols(grad_qkv, qkv_full)
    normalize_before_attention, gradient_attention_gain, gradient_attention_shift = (
        normalize_pullback(
            gradient_attention_branch,
            attention_norm_gain,
            attention_centered_scaled,
            attention_inverse_deviation,
        )
    )
    grad_base = (grad_middle + normalize_before_attention).astype(jnp.bfloat16)
    inverse_slot = (
        jnp.zeros((patch_count,), jnp.int32)
        .at[arrived_slot]
        .set(jnp.arange(patch_count, dtype=jnp.int32))
    )
    grad_global = grad_base.reshape(patch_count, PATCH, model_width)[inverse_slot].reshape(
        row_count, model_width
    )
    sent_back = lax.all_to_all(grad_base, "fsdp", split_axis=0, concat_axis=0, tiled=True)
    grad_input = unpack_rows(sent_back)
    owned = (
        lax.psum_scatter(
            gradient_attention_gain.astype(jnp.bfloat16), "fsdp", scatter_dimension=0, tiled=True
        ).astype(jnp.float32),
        lax.psum_scatter(
            gradient_attention_shift.astype(jnp.bfloat16), "fsdp", scatter_dimension=0, tiled=True
        ).astype(jnp.float32),
        lax.psum_scatter(
            grad_qkv_full.astype(jnp.bfloat16), "fsdp", scatter_dimension=0, tiled=True
        ).astype(jnp.float32),
        lax.psum_scatter(
            grad_outproj.astype(jnp.bfloat16), "fsdp", scatter_dimension=0, tiled=True
        ).astype(jnp.float32),
        lax.psum_scatter(
            gradient_feedforward_gain.astype(jnp.bfloat16), "fsdp", scatter_dimension=0, tiled=True
        ).astype(jnp.float32),
        lax.psum_scatter(
            gradient_feedforward_shift.astype(jnp.bfloat16), "fsdp", scatter_dimension=0, tiled=True
        ).astype(jnp.float32),
        lax.psum_scatter(
            grad_expand.astype(jnp.bfloat16), "fsdp", scatter_dimension=0, tiled=True
        ).astype(jnp.float32),
        lax.psum_scatter(
            grad_expand_bias.astype(jnp.bfloat16), "fsdp", scatter_dimension=0, tiled=True
        ).astype(jnp.float32),
        lax.psum_scatter(
            grad_reduce.astype(jnp.bfloat16), "fsdp", scatter_dimension=0, tiled=True
        ).astype(jnp.float32),
        lax.psum_scatter(
            grad_reduce_bias.astype(jnp.bfloat16), "fsdp", scatter_dimension=0, tiled=True
        ).astype(jnp.float32),
    )
    totals = (
        lax.psum(owned[0].astype(jnp.bfloat16), "replica").astype(jnp.float32),
        lax.psum(owned[1].astype(jnp.bfloat16), "replica").astype(jnp.float32),
        lax.psum(owned[2].astype(jnp.bfloat16), "replica").astype(jnp.float32),
        lax.psum(owned[3].astype(jnp.bfloat16), "replica").astype(jnp.float32),
        lax.psum(owned[4].astype(jnp.bfloat16), "replica").astype(jnp.float32),
        lax.psum(owned[5].astype(jnp.bfloat16), "replica").astype(jnp.float32),
        lax.psum(owned[6].astype(jnp.bfloat16), "replica").astype(jnp.float32),
        lax.psum(owned[7].astype(jnp.bfloat16), "replica").astype(jnp.float32),
        lax.psum(owned[8].astype(jnp.bfloat16), "replica").astype(jnp.float32),
        lax.psum(owned[9].astype(jnp.bfloat16), "replica").astype(jnp.float32),
    )
    return (
        layer_out,
        grad_input,
        grad_global,
        totals[0],
        totals[1],
        totals[2],
        totals[3],
        totals[4],
        totals[5],
        totals[6],
        totals[7],
        totals[8],
        totals[9],
    )


def solution(mesh):
    in_specs = (
        P(("replica", "fsdp"), None),
        P(("replica", "fsdp"), None),
        P(("replica", "fsdp"), None),
        P("replica", None),
        P("replica", None),
        P("replica", "fsdp"),
        P("fsdp"),
        P("fsdp"),
        P("fsdp", None),
        P("fsdp", None),
        P("fsdp"),
        P("fsdp"),
        P("fsdp", None),
        P("fsdp"),
        P("fsdp", None),
        P("fsdp"),
    )
    out_specs = (
        P(("replica", "fsdp"), None),
        P(("replica", "fsdp"), None),
        P(("replica", "fsdp"), None),
        P("fsdp"),
        P("fsdp"),
        P("fsdp", None),
        P("fsdp", None),
        P("fsdp"),
        P("fsdp"),
        P("fsdp", None),
        P("fsdp"),
        P("fsdp", None),
        P("fsdp"),
    )
    return jax.shard_map(body, mesh=mesh, in_specs=in_specs, out_specs=out_specs, check_vma=False)
```

profile of v0, /device:TPU:0, one launch (start us, length us, event | category | flops | bytes accessed | tf_op | source)
XLA Modules:
  0.0 805.4 jit_solution(18170484477021151799)
XLA Ops:
  14.1 7.3 all-to-all-start.1
  23.3 4.5 all-to-all-done.1
  27.8 3.6 all-to-all-start
  34.2 50.6 %all-reduce.12 = (bf16[768]{0:T(1024)(128)(2,1)S(1)}, bf16[768]{0:T(1024)(128)(2,1)S(1)}, bf16[768]{0:T(1024)(128)(2,1)S(1)}, bf16[768]{0:T(1024)(128)(2,1)S(1)}) all-reduce(bf16[768]{0:T(1024)(128)(2,1)S(1)} %dynamic-update-slice.1, bf16[768]{0:T(1024)(128)(2,1)S(1)} %dynamic-update-slice, ...), channel_id=1, replica_groups=mesh['replica'=4,'fsdp'=8] {'fsdp'}, use_global_device_ids=true, to_apply=%add.1 | all-reduce | flops 3072 | bytes 12288
  84.8 43.5 %all-gather = bf16[8,1,384]{2,1,0:T(2,128)(2,1)S(1)} all-gather(bf16[1,1,384]{2,1,0:T(2,128)(2,1)S(1)} %reshape.552), channel_id=1, replica_groups=mesh['replica'=4,'fsdp'=8] {'fsdp'}, dimensions={0}, use_global_device_ids=true | all-gather | bytes 6912 | tf_op jit(solution)/shard_map/all_gather | solution.py:134
  133.9 2.1 gather_fusion.2
  135.9 2.1 convert_element_type.224
  138.0 4.3 all-to-all-start.3
  142.4 2.4 fusion.32
  146.5 3.0 add_convert_fusion.3
  149.5 6.3 convolution_convert_fusion
  157.2 2.8 copy.85
  160.1 3.0 copy.109
  164.7 3.1 copy.108
  177.7 3.9 fusion.60
  183.8 60.6 %all-gather.10.cloned.1.call-done = bf16[768,3072]{1,0:T(8,128)(2,1)} async-done(((bf16[96,3072]{1,0:T(8,128)(2,1)}), bf16[768,3072]{1,0:T(8,128)(2,1)}) %all-gather.10.cloned.1.call-update) | async-done | bytes 4718608 | tf_op jit(solution)/shard_map/all_gather | solution.py:133
  244.4 37.7 %fusion.2 = (bf16[1024,3072]{1,0:T(8,128)(2,1)}, f32[1024,3072]{1,0:T(8,128)}) fusion(f32[3072]{0:T(1024)S(1)} %bitcast.199, bf16[768,3072]{1,0:T(8,128)(2,1)} %all-gather.10.cloned.1.call-done, f32[1024,768]{1,0:T(8,128)} %copy-done.10, f32[768]{0:T(1024)S(1)} %convert_element_type.192, f32[768]{0:T(1024)S(1)} %convert_element_type.191, ...), kind=kOutput, calls=%fused_computation.12 | convolution fusion | flops 5043388416 | bytes 26765312 | tf_op jit(solution)/shard_map/dot_general | solution.py:179
  282.1 42.4 %all-gather.12.cloned.1.call-done = bf16[3072,768]{1,0:T(8,128)(2,1)} async-done(((bf16[384,768]{1,0:T(8,128)(2,1)}), bf16[3072,768]{1,0:T(8,128)(2,1)}) %all-gather.12.cloned.1.call-update) | async-done | bytes 4718608 | tf_op jit(solution)/shard_map/all_gather | solution.py:135
  324.5 12.5 %fusion.61 = (bf16[3072]{0:T(1024)(128)(2,1)S(1)}, bf16[1024,3072]{1,0:T(8,128)(2,1)S(1)}) fusion(f32[1024,3072]{1,0:T(8,128)} %get-tuple-element.60, f32[3072]{0:T(1024)S(1)} %bitcast.200, bf16[1024,768]{1,0:T(8,128)(2,1)} %bitcast.25, bf16[3072,768]{1,0:T(8,128)(2,1)} %all-gather.12.cloned.1.call-done), kind=kOutput, calls=%fused_computation.152 | convolution fusion | flops 4869583872 | bytes 25184256 | tf_op jit(solution)/shard_map/dot_general | solution.py:19
  337.1 5.7 multiply_reduce_fusion.1
  342.8 2.4 multiply_add_fusion
  346.9 2.4 fusion.23
  349.3 3.3 convolution_convert_fusion.4
  354.8 5.0 multiply_reduce_fusion
  359.8 2.0 multiply_convert_fusion.1
  363.4 3.5 fusion.27
  367.2 4.8 fusion.28
  374.5 5.0 fusion.29
  381.9 2.2 copy-done.20
  384.2 5.5 convolution_convert_fusion.3
  390.1 10.4 %convolution_convert_fusion.2 = bf16[768,3072]{1,0:T(8,128)(2,1)} fusion(bf16[1024,3072]{1,0:T(8,128)(2,1)} %copy-done.43, f32[1024,768]{1,0:T(8,128)} %copy-done.10, f32[768]{0:T(1024)S(1)} %convert_element_type.192, f32[768]{0:T(1024)S(1)} %convert_element_type.191, f32[1024]{0:T(1024)S(1)} %add_rsqrt_fusion, f32[1024]{0:T(1024)S(1)} %broadcast_multiply_fusion.4), kind=kOutput, calls=%fused_computation.38 | convolution fusion | flops 4838129664 | bytes 14170112 | tf_op jit(solution)/shard_map/dot_general | solution.py:13
  400.6 9.1 %convolution_convert_fusion.1 = bf16[3072,768]{1,0:T(8,128)(2,1)} fusion(bf16[1024,3072]{1,0:T(8,128)(2,1)} %get-tuple-element.59, bf16[1024,768]{1,0:T(8,128)(2,1)} %bitcast.25), kind=kOutput, calls=%fused_computation.37 | convolution fusion | flops 4834197504 | bytes 12582912 | tf_op jit(solution)/shard_map/dot_general | solution.py:13
  412.5 9.6 %multiply_reduce_fusion.2 = (bf16[768]{0:T(1024)(128)(2,1)S(1)}, f32[1024]{0:T(1024)S(1)}, f32[1024]{0:T(1024)S(1)}, bf16[768]{0:T(1024)(128)(2,1)S(1)}, f32[1024,768]{1,0:T(8,128)}) fusion(f32[1024]{0:T(1024)S(1)} %copy-done.26, f32[1024]{0:T(1024)S(1)} %copy-done.22, bf16[128,8,768]{2,1,0:T(8,128)(2,1)S(1)} %copy-done.8, ...), kind=kOutput, calls=%fused_computation.45 | convolution fusion | flops 3633312256 | bytes 14571520 | tf_op jit(solution)/shard_map/dot_general | solution.py:19
  422.1 35.5 %all-reduce.11 = (bf16[768]{0:T(1024)(128)(2,1)S(1)}, bf16[768]{0:T(1024)(128)(2,1)S(1)}, bf16[768]{0:T(1024)(128)(2,1)S(1)}, bf16[768]{0:T(1024)(128)(2,1)S(1)}...) all-reduce(bf16[768]{0:T(1024)(128)(2,1)S(1)} %dynamic-update-slice, ...), channel_id=1, replica_groups=mesh['replica'=4,'fsdp'=8] {'fsdp'}, use_global_device_ids=true, to_apply=%add.4 | all-reduce | flops 7680 | bytes 30720
  457.7 9.9 %add_convert_fusion.1 = bf16[1024,768]{1,0:T(8,128)(2,1)} fusion(f32[1024,768]{1,0:T(8,128)} %copy-done.10, bf16[1024,3072]{1,0:T(8,128)(2,1)} %get-tuple-element.59, bf16[3072,768]{1,0:T(8,128)(2,1)} %all-gather.12.cloned.1.call-done, f32[768]{0:T(1024)S(1)} %convert_element_type.196), kind=kOutput, calls=%fused_computation.53 | convolution fusion | flops 4834197504 | bytes 15731712 | tf_op jit(solution)/shard_map/dot_general | solution.py:185
  467.6 4.3 all-to-all-start.2
  471.9 4.4 add_convert_fusion
  476.4 28.1 %all-to-all-done.2 = bf16[8,128,768]{2,1,0:T(8,128)(2,1)} async-done(((bf16[8,128,768]{2,1,0:T(8,128)(2,1)}), bf16[8,128,768]{2,1,0:T(8,128)(2,1)}, u32[]{:S(2)}, u32[]{:S(2)}) %all-to-all-start.2) | async-done | bytes 1572896 | tf_op jit(solution)/shard_map/all_to_all | solution.py:188
  504.4 3.7 all-to-all-start.4
  508.2 30.2 %reduce-scatter.5.cloned.1.call-done = bf16[96,2304]{1,0:T(8,128)(2,1)} async-done(((bf16[768,2304]{1,0:T(8,128)(2,1)}), bf16[96,2304]{1,0:T(8,128)(2,1)}) %reduce-scatter.5.cloned.1.call-update) | async-done | bytes 442384 | tf_op jit(solution)/shard_map/reduce_scatter | solution.py:276
  538.4 105.4 %reduce-scatter.9.cloned.1.call-done = bf16[96,3072]{1,0:T(8,128)(2,1)} async-done(((bf16[768,3072]{1,0:T(8,128)(2,1)}), bf16[96,3072]{1,0:T(8,128)(2,1)}) %reduce-scatter.9.cloned.1.call-update) | async-done | bytes 589840 | tf_op jit(solution)/shard_map/reduce_scatter | solution.py:288
  643.8 98.9 %reduce-scatter.11.cloned.1.call-done = bf16[384,768]{1,0:T(8,128)(2,1)} async-done(((bf16[3072,768]{1,0:T(8,128)(2,1)}), bf16[384,768]{1,0:T(8,128)(2,1)}) %reduce-scatter.11.cloned.1.call-update) | async-done | bytes 589840 | tf_op jit(solution)/shard_map/reduce_scatter | solution.py:294
  745.6 6.8 all-reduce.13
  757.4 3.2 gather_fusion.3
  762.4 2.9 bitcast_select_fusion
  765.3 26.4 %all-reduce.17.cloned.1.call-done = (bf16[96,2304]{1,0:T(8,128)(2,1)}, bf16[96,768]{1,0:T(8,128)(2,1)}, bf16[96,3072]{1,0:T(8,128)(2,1)}, bf16[384,768]{1,0:T(8,128)(2,1)}) async-done(((bf16[96,2304]{1,0:T(8,128)(2,1)}, bf16[96,768]{1,0:T(8,128)(2,1)}, bf16[96,3072]{1,0:T(8,128)(2,1)}, bf16[384,768]{1,0:T(8,128)(2,1)}), (bf16[96,2304]{1,0:T(8,128)(2,1)}, bf16[96,768]{1,0:T(8,128)(2,1)}, ...) | async-done | bytes 1769488 | tf_op jit(solution)/shard_map/psum | solution.py:304
  791.7 2.0 convert_element_type.210
  795.4 2.2 convert_element_type.218
  (210 shorter events, 57.9 us)
Async XLA Ops:
  7.2 14.2 %copy-start = (bf16[1024,768]{1,0:T(8,128)(2,1)S(1)}, bf16[1024,768]{1,0:T(8,128)(2,1)}, u32[]{:S(2)}) copy-start(bf16[1024,768]{1,0:T(8,128)(2,1)} %param.16) | copy-start | bytes 4718596
  7.2 142.3 %all-gather.6.cloned.1.call-start = ((), (), s32[]{:S(2)}) async-start(), calls=%async_computation.9 | async-start | bytes 3981312 | tf_op jit(solution)/shard_map/all_gather | solution.py:129
  7.9 169.8 %all-gather.8.cloned.1.call-start = ((), (), s32[]{:S(2)}) async-start(), calls=%async_computation.10 | async-start | bytes 1327104 | tf_op jit(solution)/shard_map/all_gather | solution.py:130
  8.7 235.7 %all-gather.10.cloned.1.call-start = ((), (), s32[]{:S(2)}) async-start(), calls=%async_computation.11 | async-start | bytes 5308416 | tf_op jit(solution)/shard_map/all_gather | solution.py:133
  14.1 13.7 %all-to-all-start.1 = ((s32[8,16,1]{1,2,0:T(1,128)}), s32[8,16,1]{1,2,0:T(1,128)S(1)}, u32[]{:S(2)}, u32[]{:S(2)}) async-start(s32[8,16,1]{1,2,0:T(1,128)} %bitcast.11), calls=%async_computation.1 | async-start | bytes 8192 | tf_op jit(solution)/shard_map/all_to_all | solution.py:113
  21.4 10.6 %copy-start.29 = (u32[32]{0:T(128)S(1)}, u32[32]{0:T(128)}, u32[]{:S(2)}) copy-start(u32[32]{0:T(128)} %constant.168) | copy-start | bytes 388
  21.4 11.8 %copy-start.37 = (bf16[96]{0:T(256)(128)(2,1)S(1)}, bf16[96]{0:T(256)(128)(2,1)}, u32[]{:S(2)}) copy-start(bf16[96]{0:T(256)(128)(2,1)} %param.23) | copy-start | bytes 580
  21.4 12.1 %copy-start.38 = (bf16[96]{0:T(256)(128)(2,1)S(1)}, bf16[96]{0:T(256)(128)(2,1)}, u32[]{:S(2)}) copy-start(bf16[96]{0:T(256)(128)(2,1)} %param.22) | copy-start | bytes 580
  21.5 12.3 %copy-start.39 = (bf16[96]{0:T(256)(128)(2,1)S(1)}, bf16[96]{0:T(256)(128)(2,1)}, u32[]{:S(2)}) copy-start(bf16[96]{0:T(256)(128)(2,1)} %param.27) | copy-start | bytes 580
  21.5 12.5 %copy-start.40 = (bf16[96]{0:T(256)(128)(2,1)S(1)}, bf16[96]{0:T(256)(128)(2,1)}, u32[]{:S(2)}) copy-start(bf16[96]{0:T(256)(128)(2,1)} %param.26) | copy-start | bytes 580
  21.5 63.3 %copy-start.30 = (bf16[384]{0:T(512)(128)(2,1)S(1)}, bf16[384]{0:T(512)(128)(2,1)}, u32[]{:S(2)}) copy-start(bf16[384]{0:T(512)(128)(2,1)} %param.29) | copy-start | bytes 2308
  21.5 106.8 %copy-start.41 = (s32[1,4]{1,0:T(1,128)S(1)}, s32[1,4]{1,0:T(1,128)}, u32[]{:S(2)}) copy-start(s32[1,4]{1,0:T(1,128)} %param.19) | copy-start | bytes 52
  21.5 107.1 %copy-start.31 = (s32[1,4]{1,0:T(1,128)S(1)}, s32[1,4]{1,0:T(1,128)}, u32[]{:S(2)}) copy-start(s32[1,4]{1,0:T(1,128)} %param.20) | copy-start | bytes 52
  27.8 110.2 %all-to-all-start = ((bf16[8,128,768]{2,1,0:T(8,128)(2,1)}), bf16[8,128,768]{2,1,0:T(8,128)(2,1)S(1)}, u32[]{:S(2)}, u32[]{:S(2)}) async-start(bf16[8,128,768]{2,1,0:T(8,128)(2,1)} %bitcast.8), calls=%async_computation | async-start | bytes 3145728 | tf_op jit(solution)/shard_map/all_to_all | solution.py:112
  31.4 293.1 %all-gather.12.cloned.1.call-start = ((), (), s32[]{:S(2)}) async-start(), calls=%async_computation.12 | async-start | bytes 5308416 | tf_op jit(solution)/shard_map/all_gather | solution.py:135
  84.8 61.1 %copy-start.23 = (f32[768]{0:T(1024)}, f32[768]{0:T(1024)S(1)}, u32[]{:S(2)}) copy-start(f32[768]{0:T(1024)S(1)} %convert_element_type.183) | copy-start | bytes 9220
  128.9 3.6 copy-start.27
  133.8 4.2 copy-start.34
  135.9 10.0 %copy-start.7 = (bf16[128,8,768]{2,1,0:T(8,128)(2,1)}, bf16[128,8,768]{2,1,0:T(8,128)(2,1)S(1)}, u32[]{:S(2)}) copy-start(bf16[128,8,768]{2,1,0:T(8,128)(2,1)S(1)} %gather_fusion.2) | copy-start | bytes 4718596
  138.0 7.9 copy-start.3
  138.0 144.1 %all-to-all-start.3 = ((bf16[8,128,768]{2,1,0:T(8,128)(2,1)}), bf16[8,128,768]{2,1,0:T(8,128)(2,1)}, u32[]{:S(2)}, u32[]{:S(2)}) async-start(bf16[8,128,768]{2,1,0:T(8,128)(2,1)} %bitcast.186), calls=%async_computation.3 | async-start | bytes 3145728 | tf_op jit(solution)/shard_map/all_to_all | solution.py:193
  142.3 365.8 %reduce-scatter.7.cloned.1.call-start = ((), (), s32[]{:S(2)}) async-start(), calls=%async_computation.14 | async-start | bytes 1327104 | tf_op jit(solution)/shard_map/reduce_scatter | solution.py:279
  142.4 2.8 copy-start.5
  169.1 5.1 copy-start.16
  172.6 2.6 copy-start.2
  324.5 12.5 %copy-start.11 = (f32[1024,768]{1,0:T(8,128)S(1)}, f32[1024,768]{1,0:T(8,128)}, u32[]{:S(2)}) copy-start(f32[1024,768]{1,0:T(8,128)} %copy-done.10) | copy-start | bytes 9437188
  324.5 12.6 %copy-start.35 = (bf16[768,3072]{1,0:T(8,128)(2,1)S(1)}, bf16[768,3072]{1,0:T(8,128)(2,1)}, u32[]{:S(2)}) copy-start(bf16[768,3072]{1,0:T(8,128)(2,1)} %all-gather.10.cloned.1.call-done) | copy-start | bytes 14155780
  337.0 5.7 copy-start.43
  353.8 5.9 slice-start
  354.8 5.0 slice-start.1
  367.0 5.0 copy-start.15
  367.0 171.4 %reduce-scatter.5.cloned.1.call-start = ((), (), s32[]{:S(2)}) async-start(), calls=%async_computation.13 | async-start | bytes 3981312 | tf_op jit(solution)/shard_map/reduce_scatter | solution.py:276
  381.1 3.0 copy-start.18
  389.7 254.1 %reduce-scatter.9.cloned.1.call-start = ((), (), s32[]{:S(2)}) async-start(), calls=%async_computation.15 | async-start | bytes 5308416 | tf_op jit(solution)/shard_map/reduce_scatter | solution.py:288
  400.6 342.1 %reduce-scatter.11.cloned.1.call-start = ((), (), s32[]{:S(2)}) async-start(), calls=%async_computation.16 | async-start | bytes 5308416 | tf_op jit(solution)/shard_map/reduce_scatter | solution.py:294
  409.7 2.7 copy-start.4
  409.7 2.7 copy-start.8
  409.8 2.7 copy-start.22
  409.8 2.7 copy-start.24
  409.8 2.7 copy-start.26
  467.6 36.8 %all-to-all-start.2 = ((bf16[8,128,768]{2,1,0:T(8,128)(2,1)}), bf16[8,128,768]{2,1,0:T(8,128)(2,1)}, u32[]{:S(2)}, u32[]{:S(2)}) async-start(bf16[8,128,768]{2,1,0:T(8,128)(2,1)} %bitcast.195), calls=%async_computation.2 | async-start | bytes 3145728 | tf_op jit(solution)/shard_map/all_to_all | solution.py:188
  476.3 267.6 %copy-start.33 = (s32[128]{0:T(128)S(1)}, s32[128]{0:T(128)}, u32[]{:S(2)}) copy-start(s32[128]{0:T(128)} %copy-done.32) | copy-start | bytes 1540
  476.3 279.2 %copy-start.9 = (bf16[1024,768]{1,0:T(8,128)(2,1)S(1)}, bf16[1024,768]{1,0:T(8,128)(2,1)}, u32[]{:S(2)}) copy-start(bf16[1024,768]{1,0:T(8,128)(2,1)} %add_convert_fusion) | copy-start | bytes 4718596
  504.4 256.2 %all-to-all-start.4 = ((bf16[8,128,768]{2,1,0:T(8,128)(2,1)}), bf16[8,128,768]{2,1,0:T(8,128)(2,1)S(1)}, u32[]{:S(2)}, u32[]{:S(2)}) async-start(bf16[8,128,768]{2,1,0:T(8,128)(2,1)} %bitcast.174), calls=%async_computation.4 | async-start | bytes 3145728 | tf_op jit(solution)/shard_map/all_to_all | solution.py:267
  508.1 283.6 %all-reduce.17.cloned.1.call-start = ((), (), s32[]{:S(2)}) async-start(), calls=%async_computation.17 | async-start | bytes 3538944 | tf_op jit(solution)/shard_map/psum | solution.py:304
  757.4 5.0 copy-start.28
  762.4 36.2 %copy-start.1 = (bf16[1024,768]{1,0:T(8,128)(2,1)S(1)}, bf16[1024,768]{1,0:T(8,128)(2,1)}, u32[]{:S(2)}) copy-start(bf16[1024,768]{1,0:T(8,128)(2,1)} %param.16) | copy-start | bytes 4718596
  791.7 5.9 copy-start.19
  (12 other events, 18.3 us)
Sparse Core Ops, SparseCore 0:
  10.2 92.3 all-gather.5
  104.8 45.2 all-gather.7
  152.3 92.0 all-gather.9
  246.4 78.0 all-gather.11
  367.1 62.1 reduce-scatter.6
  432.8 105.5 reduce-scatter.4
  542.0 101.7 reduce-scatter.8
  647.4 95.2 reduce-scatter.10
  745.3 46.3 all-reduce.16
where the time goes:
time: 813 us; the launch traced here: 805 us
  waiting for transfers between devices  399 us (49%)
  matrix products  137 us (17%)
  blocking collectives  136 us (17%)
  local copies, waits for them, and re-layouts  52.6 us (6%)
  other arithmetic  38.7 us (5%)
  starting transfers between devices  24.1 us (3%)
  between operations  16.9 us (2%)
    reduce_scatter x1, waiting for transfers between devices, body(): lax.psum_scatter(grad_expand.astype(jnp.bfloat16), 'fsdp', scatter_dimens...  105 us
    reduce_scatter x1, waiting for transfers between devices, body(): lax.psum_scatter(grad_reduce.astype(jnp.bfloat16), 'fsdp', scatter_dimens...  98.9 us
    unnamed x2, blocking collectives  86.1 us
    all_gather x1, waiting for transfers between devices, body(): lax.all_gather(up_weight, 'fsdp', axis=0, tiled=True)  60.6 us
    all_gather x1, blocking collectives, body(): lax.all_gather(up_bias, 'fsdp', axis=0, tiled=True)  43.5 us
    all_gather x1, waiting for transfers between devices, body(): lax.all_gather(down_weight, 'fsdp', axis=0, tiled=True)  42.4 us
    dot_general x1, matrix products, body(): jnp.dot(second_in, expand_full, preferred_element_type=jnp.float32)  37.7 us
    dot_general x4, matrix products, contract_cols(): lax.dot_general(left, right, (((1,), (1,)), ((), ())), preferred_element_...  31.2 us
  transfers between devices with their start and end apart: 14, of which 8 were waited for; matrix products, arithmetic and copies ran while one was open for 21% of the time, Pallas kernels for 0%

commit v1 on v0

--- a/solution.py
+++ b/solution.py
@@ -185,9 +185,19 @@
         + jnp.dot(activ, reduce_full, preferred_element_type=jnp.float32)
         + reduce_bias.astype(jnp.float32)
     )
-    returned = lax.all_to_all(
-        result.astype(jnp.bfloat16), "fsdp", split_axis=0, concat_axis=0, tiled=True
-    )
+    x = result.astype(jnp.bfloat16)
+    ways, here = (lax.axis_size("fsdp"), lax.axis_index("fsdp"))
+    width = x.shape[0] // ways
+    lengths = list(x.shape)
+    lengths[0] = width
+    height = lengths[0]
+    lengths[0] = height * ways
+    returned = jnp.zeros(lengths, x.dtype)
+    for mask in range(ways):
+        part = lax.dynamic_slice_in_dim(x, (here ^ mask) * width, width, axis=0)
+        if mask:
+            part = lax.ppermute(part, "fsdp", [(d, d ^ mask) for d in range(ways)])
+        returned = lax.dynamic_update_slice_in_dim(returned, part, (here ^ mask) * height, axis=0)
     layer_out = jnp.where(keep_byte, unpack_rows(returned), jnp.zeros((), jnp.bfloat16))
     masked_cot = jnp.where(keep_byte, cotangent, jnp.zeros((), jnp.bfloat16))
     upstream_b = lax.all_to_all(

time: 813 us -> 811 us (level)
  waiting for transfers between devices: 399 us -> 374 us
  local copies, waits for them, and re-layouts: 52.6 us -> 67.8 us
    all_to_all x1 -> x0, waiting for transfers between devices: 28.1 us -> none  [body(): lax.all_to_all(result.astype(jnp.bfloat16), 'fsdp', split_axis=0, concat_...]
    ppermute x0 -> x7, starting transfers between devices: none -> 11.1 us  [body(): part = lax.ppermute(part, 'fsdp', [(d, d ^ mask) for d in range(ways)])]
    psum x1, waiting for transfers between devices: 26.4 us -> 37.5 us  [body(): lax.psum(owned[2].astype(jnp.bfloat16), 'replica').astype(jnp.float32)]
    dynamic_update_slice x0 -> x7, local copies, waits for them, and re-layouts: none -> 9.48 us  [body(): lax.dynamic_update_slice_in_dim(returned, part, (here ^ mask) * height, a...]
    reduce_scatter x1, waiting for transfers between devices: 105 us -> 97.3 us  [body(): lax.psum_scatter(grad_expand.astype(jnp.bfloat16), 'fsdp', scatter_dimens...]
  transfers between devices with their start and end apart: 14 -> 20, of which waited for: 8 -> 7; matrix products, arithmetic and copies ran while one was open for 21% -> 23% of each run, Pallas kernels for 0% -> 0%
where the time goes in v1:
time: 811 us; the launch traced here: 803 us
  waiting for transfers between devices  374 us (46%)
  blocking collectives  137 us (17%)
  matrix products  137 us (17%)
  local copies, waits for them, and re-layouts  67.8 us (8%)
  other arithmetic  40.3 us (5%)
  starting transfers between devices  30.9 us (4%)
  between operations  17.3 us (2%)
    reduce_scatter x1, waiting for transfers between devices, body(): lax.psum_scatter(grad_reduce.astype(jnp.bfloat16), 'fsdp', scatter_dimens...  98.8 us
    reduce_scatter x1, waiting for transfers between devices, body(): lax.psum_scatter(grad_expand.astype(jnp.bfloat16), 'fsdp', scatter_dimens...  97.3 us
    unnamed x2, blocking collectives  86.4 us
    all_gather x1, waiting for transfers between devices, body(): lax.all_gather(up_weight, 'fsdp', axis=0, tiled=True)  60.6 us
    all_gather x1, blocking collectives, body(): lax.all_gather(up_bias, 'fsdp', axis=0, tiled=True)  43.4 us
    all_gather x1, waiting for transfers between devices, body(): lax.all_gather(down_weight, 'fsdp', axis=0, tiled=True)  42.3 us
    dot_general x1, matrix products, body(): jnp.dot(second_in, expand_full, preferred_element_type=jnp.float32)  37.8 us
    psum x1, waiting for transfers between devices, body(): lax.psum(owned[2].astype(jnp.bfloat16), 'replica').astype(jnp.float32)  37.5 us
  transfers between devices with their start and end apart: 20, of which 7 were waited for; matrix products, arithmetic and copies ran while one was open for 23% of the time, Pallas kernels for 0%

profile of v1, /device:TPU:0, one launch (start us, length us, event | category | flops | bytes accessed | tf_op | source)
XLA Modules:
  0.0 803.4 jit_solution(9091327388441003567)
XLA Ops:
  14.1 7.3 all-to-all-start.1
  23.3 4.5 all-to-all-done.1
  27.8 3.6 all-to-all-start
  34.2 50.6 %all-reduce.12 = (bf16[768]{0:T(1024)(128)(2,1)S(1)}, bf16[768]{0:T(1024)(128)(2,1)S(1)}, bf16[768]{0:T(1024)(128)(2,1)S(1)}, bf16[768]{0:T(1024)(128)(2,1)S(1)}) all-reduce(bf16[768]{0:T(1024)(128)(2,1)S(1)} %dynamic-update-slice.1, bf16[768]{0:T(1024)(128)(2,1)S(1)} %dynamic-update-slice, ...), channel_id=1, replica_groups=mesh['replica'=4,'fsdp'=8] {'fsdp'}, use_global_device_ids=true, to_apply=%add.1 | all-reduce | flops 3072 | bytes 12288
  84.8 43.4 %all-gather = bf16[8,1,384]{2,1,0:T(2,128)(2,1)S(1)} all-gather(bf16[1,1,384]{2,1,0:T(2,128)(2,1)S(1)} %reshape.549), channel_id=1, replica_groups=mesh['replica'=4,'fsdp'=8] {'fsdp'}, dimensions={0}, use_global_device_ids=true | all-gather | bytes 6912 | tf_op jit(solution)/shard_map/all_gather | solution.py:134
  130.6 1.8 gather_fusion.4
  133.8 2.1 gather_fusion.2
  135.9 2.0 convert_element_type.224
  138.0 4.3 all-to-all-start.2
  142.3 2.4 fusion.32
  146.5 3.0 add_convert_fusion.3
  149.4 6.3 convolution_convert_fusion
  157.2 2.8 copy.85
  160.0 3.1 copy.109
  164.8 3.0 copy.108
  177.7 3.9 fusion.60
  183.7 60.6 %all-gather.10.cloned.1.call-done = bf16[768,3072]{1,0:T(8,128)(2,1)} async-done(((bf16[96,3072]{1,0:T(8,128)(2,1)}), bf16[768,3072]{1,0:T(8,128)(2,1)}) %all-gather.10.cloned.1.call-update) | async-done | bytes 4718608 | tf_op jit(solution)/shard_map/all_gather | solution.py:133
  244.4 37.8 %fusion.2 = (bf16[1024,3072]{1,0:T(8,128)(2,1)}, f32[1024,3072]{1,0:T(8,128)}) fusion(f32[3072]{0:T(1024)S(1)} %bitcast.197, bf16[768,3072]{1,0:T(8,128)(2,1)} %all-gather.10.cloned.1.call-done, f32[1024,768]{1,0:T(8,128)} %copy-done.10, f32[768]{0:T(1024)S(1)} %convert_element_type.192, f32[768]{0:T(1024)S(1)} %convert_element_type.191, ...), kind=kOutput, calls=%fused_computation.12 | convolution fusion | flops 5043388416 | bytes 26765312 | tf_op jit(solution)/shard_map/dot_general | solution.py:179
  282.1 42.3 %all-gather.12.cloned.1.call-done = bf16[3072,768]{1,0:T(8,128)(2,1)} async-done(((bf16[384,768]{1,0:T(8,128)(2,1)}), bf16[3072,768]{1,0:T(8,128)(2,1)}) %all-gather.12.cloned.1.call-update) | async-done | bytes 4718608 | tf_op jit(solution)/shard_map/all_gather | solution.py:135
  324.5 12.5 %fusion.61 = (bf16[3072]{0:T(1024)(128)(2,1)S(1)}, bf16[1024,3072]{1,0:T(8,128)(2,1)S(1)}) fusion(f32[1024,3072]{1,0:T(8,128)} %get-tuple-element.68, f32[3072]{0:T(1024)S(1)} %bitcast.198, bf16[1024,768]{1,0:T(8,128)(2,1)} %bitcast.24, bf16[3072,768]{1,0:T(8,128)(2,1)} %all-gather.12.cloned.1.call-done), kind=kOutput, calls=%fused_computation.167 | convolution fusion | flops 4869583872 | bytes 25184256 | tf_op jit(solution)/shard_map/dot_general | solution.py:19
  337.0 5.7 multiply_reduce_fusion.1
  342.7 2.4 multiply_add_fusion
  346.8 2.4 fusion.23
  349.2 3.3 convolution_convert_fusion.4
  354.7 5.0 multiply_reduce_fusion
  359.7 2.0 multiply_convert_fusion.1
  363.4 3.5 fusion.27
  367.2 4.8 fusion.28
  374.4 5.0 fusion.29
  381.9 2.2 copy-done.20
  384.0 5.4 convolution_convert_fusion.3
  390.0 10.5 %convolution_convert_fusion.2 = bf16[768,3072]{1,0:T(8,128)(2,1)} fusion(bf16[1024,3072]{1,0:T(8,128)(2,1)} %copy-done.43, f32[1024,768]{1,0:T(8,128)} %copy-done.10, f32[768]{0:T(1024)S(1)} %convert_element_type.192, f32[768]{0:T(1024)S(1)} %convert_element_type.191, f32[1024]{0:T(1024)S(1)} %add_rsqrt_fusion, f32[1024]{0:T(1024)S(1)} %broadcast_multiply_fusion.4), kind=kOutput, calls=%fused_computation.38 | convolution fusion | flops 4838129664 | bytes 14170112 | tf_op jit(solution)/shard_map/dot_general | solution.py:13
  400.6 9.2 %convolution_convert_fusion.1 = bf16[3072,768]{1,0:T(8,128)(2,1)} fusion(bf16[1024,3072]{1,0:T(8,128)(2,1)} %get-tuple-element.67, bf16[1024,768]{1,0:T(8,128)(2,1)} %bitcast.24), kind=kOutput, calls=%fused_computation.37 | convolution fusion | flops 4834197504 | bytes 12582912 | tf_op jit(solution)/shard_map/dot_general | solution.py:13
  414.6 9.8 %multiply_reduce_fusion.2 = (bf16[768]{0:T(1024)(128)(2,1)S(1)}, f32[1024]{0:T(1024)S(1)}, f32[1024]{0:T(1024)S(1)}, bf16[768]{0:T(1024)(128)(2,1)S(1)}, f32[1024,768]{1,0:T(8,128)}) fusion(f32[1024]{0:T(1024)S(1)} %copy-done.26, f32[1024]{0:T(1024)S(1)} %copy-done.22, bf16[128,8,768]{2,1,0:T(8,128)(2,1)S(1)} %copy-done.8, ...), kind=kOutput, calls=%fused_computation.45 | convolution fusion | flops 3633312256 | bytes 14571520 | tf_op jit(solution)/shard_map/dot_general | solution.py:19
  424.3 35.8 %all-reduce.11 = (bf16[768]{0:T(1024)(128)(2,1)S(1)}, bf16[768]{0:T(1024)(128)(2,1)}, bf16[768]{0:T(1024)(128)(2,1)}, bf16[768]{0:T(1024)(128)(2,1)}, bf16[768]{...) all-reduce(bf16[768]{0:T(1024)(128)(2,1)S(1)} %dynamic-update-slice, ...), channel_id=1, replica_groups=mesh['replica'=4,'fsdp'=8] {'fsdp'}, use_global_device_ids=true, to_apply=%add.4 | all-reduce | flops 7680 | bytes 30720
  460.2 4.5 add_convert_fusion
  464.6 3.6 all-to-all-start.3
  468.3 9.1 %add_convert_fusion.1 = bf16[1024,768]{1,0:T(8,128)(2,1)S(1)} fusion(f32[1024,768]{1,0:T(8,128)} %copy-done.10, bf16[1024,3072]{1,0:T(8,128)(2,1)} %get-tuple-element.67, bf16[3072,768]{1,0:T(8,128)(2,1)} %all-gather.12.cloned.1.call-done, f32[768]{0:T(1024)S(1)} %convert_element_type.196), kind=kOutput, calls=%fused_computation.53 | convolution fusion | flops 4834197504 | bytes 15731712 | tf_op jit(solution)/shard_map/dot_general | solution.py:185
  483.2 2.8 collective-permute-start.3
  493.1 6.7 all-reduce.13
  508.0 3.3 collective-permute-start.5
  514.7 29.9 %reduce-scatter.5.cloned.1.call-done = bf16[96,2304]{1,0:T(8,128)(2,1)} async-done(((bf16[768,2304]{1,0:T(8,128)(2,1)}), bf16[96,2304]{1,0:T(8,128)(2,1)}) %reduce-scatter.5.cloned.1.call-update) | async-done | bytes 442384 | tf_op jit(solution)/shard_map/reduce_scatter | solution.py:286
  544.6 97.3 %reduce-scatter.9.cloned.1.call-done = bf16[96,3072]{1,0:T(8,128)(2,1)} async-done(((bf16[768,3072]{1,0:T(8,128)(2,1)}), bf16[96,3072]{1,0:T(8,128)(2,1)}) %reduce-scatter.9.cloned.1.call-update) | async-done | bytes 589840 | tf_op jit(solution)/shard_map/reduce_scatter | solution.py:298
  641.9 98.8 %reduce-scatter.11.cloned.1.call-done = bf16[384,768]{1,0:T(8,128)(2,1)} async-done(((bf16[3072,768]{1,0:T(8,128)(2,1)}), bf16[384,768]{1,0:T(8,128)(2,1)}) %reduce-scatter.11.cloned.1.call-update) | async-done | bytes 589840 | tf_op jit(solution)/shard_map/reduce_scatter | solution.py:304
  747.0 2.1 gather_fusion.3
  752.2 37.5 %all-reduce.17.cloned.1.call-done = (bf16[96,2304]{1,0:T(8,128)(2,1)}, bf16[96,768]{1,0:T(8,128)(2,1)}, bf16[96,3072]{1,0:T(8,128)(2,1)}, bf16[384,768]{1,0:T(8,128)(2,1)}) async-done(((bf16[96,2304]{1,0:T(8,128)(2,1)}, bf16[96,768]{1,0:T(8,128)(2,1)}, bf16[96,3072]{1,0:T(8,128)(2,1)}, bf16[384,768]{1,0:T(8,128)(2,1)}), (bf16[96,2304]{1,0:T(8,128)(2,1)}, bf16[96,768]{1,0:T(8,128)(2,1)}, ...) | async-done | bytes 1769488 | tf_op jit(solution)/shard_map/psum | solution.py:314
  789.7 2.0 convert_element_type.210
  793.4 2.2 convert_element_type.218
  (231 shorter events, 82.0 us)
Async XLA Ops:
  7.2 14.2 %copy-start = (bf16[1024,768]{1,0:T(8,128)(2,1)S(1)}, bf16[1024,768]{1,0:T(8,128)(2,1)}, u32[]{:S(2)}) copy-start(bf16[1024,768]{1,0:T(8,128)(2,1)} %param.16) | copy-start | bytes 4718596
  7.2 142.2 %all-gather.6.cloned.1.call-start = ((), (), s32[]{:S(2)}) async-start(), calls=%async_computation.8 | async-start | bytes 3981312 | tf_op jit(solution)/shard_map/all_gather | solution.py:129
  7.9 169.8 %all-gather.8.cloned.1.call-start = ((), (), s32[]{:S(2)}) async-start(), calls=%async_computation.9 | async-start | bytes 1327104 | tf_op jit(solution)/shard_map/all_gather | solution.py:130
  8.7 235.7 %all-gather.10.cloned.1.call-start = ((), (), s32[]{:S(2)}) async-start(), calls=%async_computation.10 | async-start | bytes 5308416 | tf_op jit(solution)/shard_map/all_gather | solution.py:133
  11.2 16.6 %copy-start.32 = (s32[128]{0:T(128)}, s32[128]{0:T(128)S(1)}, u32[]{:S(2)}) copy-start(s32[128]{0:T(128)S(1)} %fusion.49) | copy-start | bytes 1540
  14.1 13.7 %all-to-all-start.1 = ((s32[8,16,1]{1,2,0:T(1,128)}), s32[8,16,1]{1,2,0:T(1,128)S(1)}, u32[]{:S(2)}, u32[]{:S(2)}) async-start(s32[8,16,1]{1,2,0:T(1,128)} %bitcast.11), calls=%async_computation.1 | async-start | bytes 8192 | tf_op jit(solution)/shard_map/all_to_all | solution.py:113
  21.4 10.6 %copy-start.29 = (u32[32]{0:T(128)S(1)}, u32[32]{0:T(128)}, u32[]{:S(2)}) copy-start(u32[32]{0:T(128)} %constant.182) | copy-start | bytes 388
  21.4 11.8 %copy-start.37 = (bf16[96]{0:T(256)(128)(2,1)S(1)}, bf16[96]{0:T(256)(128)(2,1)}, u32[]{:S(2)}) copy-start(bf16[96]{0:T(256)(128)(2,1)} %param.23) | copy-start | bytes 580
  21.4 12.1 %copy-start.38 = (bf16[96]{0:T(256)(128)(2,1)S(1)}, bf16[96]{0:T(256)(128)(2,1)}, u32[]{:S(2)}) copy-start(bf16[96]{0:T(256)(128)(2,1)} %param.22) | copy-start | bytes 580
  21.5 12.3 %copy-start.39 = (bf16[96]{0:T(256)(128)(2,1)S(1)}, bf16[96]{0:T(256)(128)(2,1)}, u32[]{:S(2)}) copy-start(bf16[96]{0:T(256)(128)(2,1)} %param.27) | copy-start | bytes 580
  21.5 12.5 %copy-start.40 = (bf16[96]{0:T(256)(128)(2,1)S(1)}, bf16[96]{0:T(256)(128)(2,1)}, u32[]{:S(2)}) copy-start(bf16[96]{0:T(256)(128)(2,1)} %param.26) | copy-start | bytes 580
  21.5 63.3 %copy-start.30 = (bf16[384]{0:T(512)(128)(2,1)S(1)}, bf16[384]{0:T(512)(128)(2,1)}, u32[]{:S(2)}) copy-start(bf16[384]{0:T(512)(128)(2,1)} %param.29) | copy-start | bytes 2308
  21.5 106.8 %copy-start.41 = (s32[1,4]{1,0:T(1,128)S(1)}, s32[1,4]{1,0:T(1,128)}, u32[]{:S(2)}) copy-start(s32[1,4]{1,0:T(1,128)} %param.19) | copy-start | bytes 52
  21.5 107.1 %copy-start.31 = (s32[1,4]{1,0:T(1,128)S(1)}, s32[1,4]{1,0:T(1,128)}, u32[]{:S(2)}) copy-start(s32[1,4]{1,0:T(1,128)} %param.20) | copy-start | bytes 52
  27.8 110.2 %all-to-all-start = ((bf16[8,128,768]{2,1,0:T(8,128)(2,1)}), bf16[8,128,768]{2,1,0:T(8,128)(2,1)S(1)}, u32[]{:S(2)}, u32[]{:S(2)}) async-start(bf16[8,128,768]{2,1,0:T(8,128)(2,1)} %bitcast.8), calls=%async_computation | async-start | bytes 3145728 | tf_op jit(solution)/shard_map/all_to_all | solution.py:112
  31.4 293.1 %all-gather.12.cloned.1.call-start = ((), (), s32[]{:S(2)}) async-start(), calls=%async_computation.11 | async-start | bytes 5308416 | tf_op jit(solution)/shard_map/all_gather | solution.py:135
  84.8 61.1 %copy-start.23 = (f32[768]{0:T(1024)}, f32[768]{0:T(1024)S(1)}, u32[]{:S(2)}) copy-start(f32[768]{0:T(1024)S(1)} %convert_element_type.183) | copy-start | bytes 9220
  135.9 10.0 %copy-start.7 = (bf16[128,8,768]{2,1,0:T(8,128)(2,1)}, bf16[128,8,768]{2,1,0:T(8,128)(2,1)S(1)}, u32[]{:S(2)}) copy-start(bf16[128,8,768]{2,1,0:T(8,128)(2,1)S(1)} %gather_fusion.2) | copy-start | bytes 4718596
  138.0 7.9 copy-start.3
  138.0 144.2 %all-to-all-start.2 = ((bf16[8,128,768]{2,1,0:T(8,128)(2,1)}), bf16[8,128,768]{2,1,0:T(8,128)(2,1)}, u32[]{:S(2)}, u32[]{:S(2)}) async-start(bf16[8,128,768]{2,1,0:T(8,128)(2,1)} %bitcast.185), calls=%async_computation.2 | async-start | bytes 3145728 | tf_op jit(solution)/shard_map/all_to_all | solution.py:203
  142.3 372.4 %reduce-scatter.7.cloned.1.call-start = ((), (), s32[]{:S(2)}) async-start(), calls=%async_computation.13 | async-start | bytes 1327104 | tf_op jit(solution)/shard_map/reduce_scatter | solution.py:289
  169.1 5.1 copy-start.16
  324.5 12.5 %copy-start.11 = (f32[1024,768]{1,0:T(8,128)S(1)}, f32[1024,768]{1,0:T(8,128)}, u32[]{:S(2)}) copy-start(f32[1024,768]{1,0:T(8,128)} %copy-done.10) | copy-start | bytes 9437188
  324.5 12.6 %copy-start.35 = (bf16[768,3072]{1,0:T(8,128)(2,1)S(1)}, bf16[768,3072]{1,0:T(8,128)(2,1)}, u32[]{:S(2)}) copy-start(bf16[768,3072]{1,0:T(8,128)(2,1)} %all-gather.10.cloned.1.call-done) | copy-start | bytes 14155780
  337.0 5.7 copy-start.43
  353.8 5.9 slice-start
  354.7 5.0 slice-start.1
  366.9 5.0 copy-start.15
  366.9 177.7 %reduce-scatter.5.cloned.1.call-start = ((), (), s32[]{:S(2)}) async-start(), calls=%async_computation.12 | async-start | bytes 3981312 | tf_op jit(solution)/shard_map/reduce_scatter | solution.py:286
  389.5 252.3 %reduce-scatter.9.cloned.1.call-start = ((), (), s32[]{:S(2)}) async-start(), calls=%async_computation.14 | async-start | bytes 5308416 | tf_op jit(solution)/shard_map/reduce_scatter | solution.py:298
  400.5 340.2 %reduce-scatter.11.cloned.1.call-start = ((), (), s32[]{:S(2)}) async-start(), calls=%async_computation.15 | async-start | bytes 5308416 | tf_op jit(solution)/shard_map/reduce_scatter | solution.py:304
  409.7 4.8 copy-start.4
  409.7 4.8 copy-start.8
  409.7 4.8 copy-start.22
  409.8 4.8 copy-start.24
  464.6 285.8 %all-to-all-start.3 = ((bf16[8,128,768]{2,1,0:T(8,128)(2,1)}), bf16[8,128,768]{2,1,0:T(8,128)(2,1)S(1)}, u32[]{:S(2)}, u32[]{:S(2)}) async-start(bf16[8,128,768]{2,1,0:T(8,128)(2,1)} %bitcast.173), calls=%async_computation.3 | async-start | bytes 3145728 | tf_op jit(solution)/shard_map/all_to_all | solution.py:277
  468.2 321.5 %all-reduce.17.cloned.1.call-start = ((), (), s32[]{:S(2)}) async-start(), calls=%async_computation.16 | async-start | bytes 3538944 | tf_op jit(solution)/shard_map/psum | solution.py:314
  477.4 28.7 %copy-start.9 = (bf16[1024,768]{1,0:T(8,128)(2,1)S(1)}, bf16[1024,768]{1,0:T(8,128)(2,1)}, u32[]{:S(2)}) copy-start(bf16[1024,768]{1,0:T(8,128)(2,1)} %add_convert_fusion) | copy-start | bytes 4718596
  479.7 28.3 %collective-permute-start = (bf16[128,768]{1,0:T(8,128)(2,1)}, bf16[128,768]{1,0:T(8,128)(2,1)}, u32[]{:S(2)}, u32[]{:S(2)}) collective-permute-start(bf16[128,768]{1,0:T(8,128)(2,1)} %get-tuple-element.55), channel_id=1, source_target_pairs={{0,1},{1,0},{2,3},{3,2},{4,5},{5,4},{6,7},{7,6},{8,9},{9,8},{10,11... | collective-permute-start | bytes 589832 | tf_op jit(solution)/shard_map/ppermute | solution.py:199
  481.5 31.4 %collective-permute-start.1 = (bf16[128,768]{1,0:T(8,128)(2,1)}, bf16[128,768]{1,0:T(8,128)(2,1)}, u32[]{:S(2)}, u32[]{:S(2)}) collective-permute-start(bf16[128,768]{1,0:T(8,128)(2,1)} %get-tuple-element.54), channel_id=1, source_target_pairs={{0,2},{1,3},{2,0},{3,1},{4,6},{5,7},{6,4},{7,5},{8,10},{9,11},{10,... | collective-permute-start | bytes 589832 | tf_op jit(solution)/shard_map/ppermute | solution.py:199
  483.0 257.7 %collective-permute-start.2 = (bf16[128,768]{1,0:T(8,128)(2,1)}, bf16[128,768]{1,0:T(8,128)(2,1)}, u32[]{:S(2)}, u32[]{:S(2)}) collective-permute-start(bf16[128,768]{1,0:T(8,128)(2,1)} %get-tuple-element.53), channel_id=1, source_target_pairs={{0,3},{1,2},{2,1},{3,0},{4,7},{5,6},{6,5},{7,4},{8,11},{9,10},{10,... | collective-permute-start | bytes 589832 | tf_op jit(solution)/shard_map/ppermute | solution.py:199
  483.2 259.2 %collective-permute-start.3 = (bf16[128,768]{1,0:T(8,128)(2,1)}, bf16[128,768]{1,0:T(8,128)(2,1)}, u32[]{:S(2)}, u32[]{:S(2)}) collective-permute-start(bf16[128,768]{1,0:T(8,128)(2,1)} %get-tuple-element.52), channel_id=1, source_target_pairs={{0,4},{1,5},{2,6},{3,7},{4,0},{5,1},{6,2},{7,3},{8,12},{9,13},{10,... | collective-permute-start | bytes 589832 | tf_op jit(solution)/shard_map/ppermute | solution.py:199
  485.9 258.0 %collective-permute-start.4 = (bf16[128,768]{1,0:T(8,128)(2,1)}, bf16[128,768]{1,0:T(8,128)(2,1)}, u32[]{:S(2)}, u32[]{:S(2)}) collective-permute-start(bf16[128,768]{1,0:T(8,128)(2,1)} %get-tuple-element.51), channel_id=1, source_target_pairs={{0,5},{1,4},{2,7},{3,6},{4,1},{5,0},{6,3},{7,2},{8,13},{9,12},{10,... | collective-permute-start | bytes 589832 | tf_op jit(solution)/shard_map/ppermute | solution.py:199
  508.0 237.6 %collective-permute-start.5 = (bf16[128,768]{1,0:T(8,128)(2,1)S(1)}, bf16[128,768]{1,0:T(8,128)(2,1)S(1)}, u32[]{:S(2)}, u32[]{:S(2)}) collective-permute-start(bf16[128,768]{1,0:T(8,128)(2,1)S(1)} %get-tuple-element.50), channel_id=1, source_target_pairs={{0,6},{1,7},{2,4},{3,5},{4,2},{5,3},{6,0},{7,1},{8,14},{9,15},{10,... | collective-permute-start | bytes 589832 | tf_op jit(solution)/shard_map/ppermute | solution.py:199
  512.9 233.4 %collective-permute-start.6 = (bf16[128,768]{1,0:T(8,128)(2,1)S(1)}, bf16[128,768]{1,0:T(8,128)(2,1)S(1)}, u32[]{:S(2)}, u32[]{:S(2)}) collective-permute-start(bf16[128,768]{1,0:T(8,128)(2,1)S(1)} %get-tuple-element.49), channel_id=1, source_target_pairs={{0,7},{1,6},{2,5},{3,4},{4,3},{5,2},{6,1},{7,0},{8,15},{9,14},{10,... | collective-permute-start | bytes 589832 | tf_op jit(solution)/shard_map/ppermute | solution.py:199
  740.7 8.4 %copy-start.28 = (pred[1024]{0:T(1024)(128)(4,1)S(1)}, pred[1024]{0:T(1024)(128)(4,1)}, u32[]{:S(2)}) copy-start(pred[1024]{0:T(1024)(128)(4,1)} %copy-done.27) | copy-start | bytes 3076
  750.4 46.2 %copy-start.1 = (bf16[1024,768]{1,0:T(8,128)(2,1)S(1)}, bf16[1024,768]{1,0:T(8,128)(2,1)}, u32[]{:S(2)}) copy-start(bf16[1024,768]{1,0:T(8,128)(2,1)} %param.16) | copy-start | bytes 4718596
  789.7 5.9 copy-start.19
  (18 other events, 41.1 us)
Sparse Core Ops, SparseCore 0:
  10.2 92.3 all-gather.5
  104.8 45.4 all-gather.7
  152.4 91.8 all-gather.9
  246.4 78.0 all-gather.11
  367.0 62.1 reduce-scatter.6
  432.7 111.8 reduce-scatter.4
  548.2 93.5 reduce-scatter.8
  645.5 95.1 reduce-scatter.10
  743.3 46.3 all-reduce.16
